TPU v7x, 32 devices: a whole 2x2x4 slice. The times are simulated.
32 devices in a mesh: grp: 2 (over core), blk: 16 (over z, y, x).
Axes of the slice: x: 2, y: 2, z: 4, core: 2. Of those that a mesh axis runs over, the one named last changes fastest.
Arguments:
- src_feats: bfloat16 [2, 4096, 512], P('grp', 'blk')
- tgt_feats: bfloat16 [2, 4096, 512], P('grp', 'blk')
- proj_weight: bfloat16 [512, 512], replicated, may hold values from -0.25 to 0.25
- match_blocks: int32 [2, 32, 4], P('grp', 'blk'), may hold values from 0 to 31, as said below
- match_count: int32 [2, 32], P('grp', 'blk'), may hold values from 1 to 4
- pair_src: int32 [2, 32, 4, 128], P('grp', 'blk'), may hold values from 0 to 127
- pair_tgt: int32 [2, 32, 4, 128], P('grp', 'blk'), may hold values from 0 to 127
Outputs:
- weight_grad: float32 [512, 512], replicated
- covariance: float32 [2, 512, 512], P('grp')
Inputs may be any that keep to these rules, and one draw needn't show every extreme that they name: `match_blocks`: each row lists 4 different target blocks; for source block s each listed block t has t // 2 at most 1 away from s // 2 along the loop of 16 runs (taken mod 16); unused slots follow the same rule.
All inputs are finite; a program needn't handle non-finite values.
Results may differ from a plain program's by a relative error of at most 0.0052.
Values may be sent and summed in bfloat16 or wider, within the bound.
No kernel may reach another device: no remote copies, remote signals or barrier semaphores. Data moves between devices by JAX's collectives and lax.ppermute only.
A program may use at most 64 MiB of HBM per device.

v0:
```python
import jax
import jax.numpy as jnp
from jax import lax
from jax.sharding import PartitionSpec as P

sharpness_divisor = 0.4
logit_bound = 2.5
norm_eps = 1e-06


def from_behind(shard, axis, by):
    count = lax.axis_size(axis)
    return lax.ppermute(shard, axis, [(i, (i + by) % count) for i in range(count)])


def project(features, weight_mat):
    projected = jnp.dot(features, weight_mat, preferred_element_type=jnp.float32)
    inv_norm = lax.rsqrt(jnp.sum(projected * projected, axis=1, keepdims=True) + norm_eps)
    unit_rows = projected * inv_norm
    return (unit_rows, inv_norm, unit_rows.astype(jnp.bfloat16))


def back_norm(unit_rows, inv_norm, grad_rows):
    inner = jnp.sum(unit_rows * grad_rows, axis=1, keepdims=True)
    return ((grad_rows - unit_rows * inner) * inv_norm).astype(jnp.bfloat16)


def pair_weights(anchor_stack, candidate_stack, onehot, matched):
    similarity_table = (
        jnp.einsum(
            "smd,skd->smk", anchor_stack, candidate_stack, preferred_element_type=jnp.float32
        )
        / sharpness_divisor
    )
    exp_terms = jnp.exp(similarity_table - logit_bound)
    shares = exp_terms / jnp.sum(exp_terms, axis=2, keepdims=True)
    linear_weights = (shares - onehot).astype(jnp.bfloat16)
    return linear_weights * matched.astype(jnp.bfloat16)[:, None, None]


def spread_blocks(target_total, linear_weights, anchor_stack, local_blocks, blocks_dev):
    slot_pieces = (
        jnp.einsum("smk,smd->skd", linear_weights, anchor_stack, preferred_element_type=jnp.float32)
        / sharpness_divisor
    )
    choice_mask = (
        local_blocks[:, None] == jnp.arange(blocks_dev, dtype=jnp.int32)[None, :]
    ).astype(jnp.float32)
    return target_total + jnp.einsum(
        "qm,qoi->moi", choice_mask, slot_pieces, precision=lax.Precision.HIGHEST
    )


def body(src_feats, tgt_feats, proj_weight, match_blocks, match_count, pair_src, pair_tgt):
    src_rows = src_feats[0]
    tgt_rows = tgt_feats[0]
    src_unit, source_inverse_norm, src_half = project(src_rows, proj_weight)
    tgt_unit, tgt_inv, tgt_half = project(tgt_rows, proj_weight)
    local_points = src_rows.shape[0]
    feature_width = src_rows.shape[1]
    blocks_dev = match_blocks.shape[1]
    slot_count = match_blocks.shape[2]
    matched_pair_count = pair_src.shape[3]
    block_points = local_points // blocks_dev
    slot_total = blocks_dev * slot_count
    runs = lax.axis_size("blk")
    reach_runs = runs // 16
    owning_run_index = lax.axis_index("blk")
    src_blocks = src_half.reshape(blocks_dev, block_points, feature_width)
    tgt_blocks = tgt_half.reshape(blocks_dev, block_points, feature_width)
    slot_index = jnp.arange(slot_count, dtype=jnp.int32)
    listed_flat = match_blocks[0].reshape(-1)
    live_flat = (slot_index[None, :] < match_count[0][:, None]).reshape(-1)
    block_base = (jnp.arange(blocks_dev, dtype=jnp.int32) * block_points)[:, None, None]
    row_index = (block_base + pair_src[0]).reshape(-1)
    tgt_table = pair_tgt[0].reshape(slot_total, matched_pair_count)
    query_stack = jnp.take(src_half, row_index, axis=0).reshape(
        slot_total, matched_pair_count, feature_width
    )
    columns = jnp.arange(block_points, dtype=jnp.int32)
    source_onehot = (tgt_table[:, :, None] == columns[None, None, :]).astype(jnp.float32)
    local_listed = listed_flat % blocks_dev
    query_zeros = jnp.zeros((slot_total * matched_pair_count, feature_width), jnp.float32)
    block_zeros = jnp.zeros((blocks_dev, block_points, feature_width), jnp.float32)

    def source_slots(held_tgt, run_id, query_total, target_total):
        matched = (listed_flat // blocks_dev == run_id) & live_flat
        candidate_stack = jnp.take(held_tgt, local_listed, axis=0)
        linear_weights = pair_weights(query_stack, candidate_stack, source_onehot, matched)
        query_part = (
            jnp.einsum(
                "smk,skd->smd", linear_weights, candidate_stack, preferred_element_type=jnp.float32
            )
            / sharpness_divisor
        )
        query_total = query_total + query_part.reshape(
            slot_total * matched_pair_count, feature_width
        )
        return (query_total, target_total)

    pair_table = jnp.concatenate(
        [pair_src[0].reshape(slot_total, matched_pair_count), tgt_table], axis=1
    )
    head_table = jnp.stack([listed_flat, live_flat.astype(jnp.int32)], axis=1)
    owner_base = (jnp.arange(slot_total, dtype=jnp.int32) // slot_count * block_points)[:, None]

    def target_slots(kept_source_rows, pair_rows, list_heads, target_total):
        target_blocks = list_heads[:, 0]
        matched = (target_blocks // blocks_dev == owning_run_index) & (list_heads[:, 1] > 0)
        their_src = pair_rows[:, :matched_pair_count]
        their_tgt = pair_rows[:, matched_pair_count:]
        gather_rows = (owner_base + their_src).reshape(-1)
        anchor_stack = jnp.take(
            kept_source_rows.reshape(local_points, feature_width), gather_rows, axis=0
        ).reshape(slot_total, matched_pair_count, feature_width)
        local_blocks = target_blocks % blocks_dev
        candidate_stack = jnp.take(tgt_blocks, local_blocks, axis=0)
        onehot = (their_tgt[:, :, None] == columns[None, None, :]).astype(jnp.float32)
        linear_weights = pair_weights(anchor_stack, candidate_stack, onehot, matched)
        return spread_blocks(target_total, linear_weights, anchor_stack, local_blocks, blocks_dev)

    def visit_run(held, run_id, totals):
        held_pair, pair_rows, list_heads = held
        query_total, target_total = totals
        query_total, _ = source_slots(held_pair[1], run_id, query_total, block_zeros)
        target_total = target_slots(held_pair[0], pair_rows, list_heads, target_total)
        return (query_total, target_total)

    own_held = (jnp.stack([src_blocks, tgt_blocks]), pair_table, head_table)
    totals = visit_run(own_held, owning_run_index, (query_zeros, block_zeros))

    def advance(offset, loop_state):
        ahead_held, behind_held, running = loop_state
        ahead_held = from_behind((ahead_held[0], ahead_held[1], ahead_held[2]), "blk", 1)
        behind_held = from_behind((behind_held[0], behind_held[1], behind_held[2]), "blk", -1)
        running = visit_run(ahead_held, (owning_run_index - offset) % runs, running)
        running = visit_run(behind_held, (owning_run_index + offset) % runs, running)
        return (ahead_held, behind_held, running)

    _, _, (anchor_loss_slope, grad_target) = lax.fori_loop(
        1, reach_runs + 1, advance, (own_held, own_held, totals)
    )
    grad_source = jax.ops.segment_sum(anchor_loss_slope, row_index, num_segments=local_points)
    src_grad = back_norm(src_unit, source_inverse_norm, grad_source)
    tgt_grad = back_norm(tgt_unit, tgt_inv, grad_target.reshape(local_points, feature_width))
    weight_part = lax.dot_general(
        src_rows, src_grad, (((0,), (0,)), ((), ())), preferred_element_type=jnp.float32
    )
    weight_part = weight_part + lax.dot_general(
        tgt_rows, tgt_grad, (((0,), (0,)), ((), ())), preferred_element_type=jnp.float32
    )
    weight_grad = lax.psum(weight_part, ("grp", "blk"))
    moment = lax.dot_general(
        src_half, src_half, (((0,), (0,)), ((), ())), preferred_element_type=jnp.float32
    )
    moment = moment + lax.dot_general(
        tgt_half, tgt_half, (((0,), (0,)), ((), ())), preferred_element_type=jnp.float32
    )
    moment = moment * (feature_width / (2.0 * local_points * runs))
    covariance = lax.psum(moment, "blk")
    return (weight_grad, covariance[None])


def solution(mesh):
    placed = (
        P("grp", "blk", None),
        P("grp", "blk", None),
        P(),
        P("grp", "blk", None),
        P("grp", "blk"),
        P("grp", "blk", None, None),
        P("grp", "blk", None, None),
    )
    return jax.shard_map(
        body, mesh=mesh, in_specs=placed, out_specs=(P(), P("grp", None, None)), check_vma=False
    )
```

profile of v0, /device:TPU:0, one launch (start us, length us, event | category | flops | bytes accessed | tf_op | source)
XLA Modules:
  0.0 379.4 jit_solution(14157346822565561980)
XLA Ops:
  8.9 7.0 %collective-permute-start.4 = (s32[8,2]{0,1:T(2,128)S(1)}, s32[8,2]{0,1:T(2,128)S(1)}, u32[]{:S(2)}, u32[]{:S(2)}) collective-permute-start(s32[8,2]{0,1:T(2,128)S(1)} %pad_add_fusion.1), channel_id=1, source_target_pairs={{0,15},{1,0},{2,1},{3,2},{4,3},{5,4},{6,5},{7,6},{8,7},{9,8},{10,9... | collective-permute-start | bytes 200 | tf_op jit(solution)/shard_map/while/body/eval_jaxpr/ppermute | solution.py:13
  16.6 5.6 %collective-permute-start.5 = (s32[8,256]{1,0:T(8,128)S(1)}, s32[8,256]{1,0:T(8,128)S(1)}, u32[]{:S(2)}, u32[]{:S(2)}) collective-permute-start(s32[8,256]{1,0:T(8,128)S(1)} %pad_add_fusion), channel_id=1, source_target_pairs={{0,15},{1,0},{2,1},{3,2},{4,3},{5,4},{6,5},{7,6},{8,7},{9,8},{10,9... | collective-permute-start | bytes 24584 | tf_op jit(solution)/shard_map/while/body/eval_jaxpr/ppermute | solution.py:13
  26.0 5.6 %collective-permute-start.1 = (bf16[2,2,128,512]{3,2,1,0:T(8,128)(2,1)}, bf16[2,2,128,512]{3,2,1,0:T(8,128)(2,1)}, u32[]{:S(2)}, u32[]{:S(2)}) collective-permute-start(bf16[2,2,128,512]{3,2,1,0:T(8,128)(2,1)} %pad_maximum_fusion), channel_id=1, source_target_pairs={{0,15},{1,0},{2,1},{3,2},{4,3},{5,4},{6,5},{7,6},{8,7},{9,8},{10,9... | collective-permute-start | bytes 1572872 | tf_op jit(solution)/shard_map/while/body/eval_jaxpr/ppermute | solution.py:13
  31.9 1.6 gather_fusion.1
  33.6 1.6 gather_fusion.8
  35.2 1.6 gather_fusion.6
  36.9 4.0 %gather_fusion.4 = bf16[1024,512]{1,0:T(8,128)(2,1)S(1)} fusion(bf16[256,512]{1,0:T(8,128)(2,1)S(1)} %multiply_convert_fusion.2, s32[1024]{0:T(1024)S(1)} %get-tuple-element.77), kind=kCustom, calls=%fused_computation.2.clone | custom fusion | bytes 2101248 | tf_op jit(solution)/shard_map/jit(_take)/gather | solution.py:113
  40.9 5.1 %gather_fusion = bf16[1024,512]{1,0:T(8,128)(2,1)} fusion(bf16[256,512]{1,0:T(8,128)(2,1)S(1)} %multiply_convert_fusion.2, s32[1024]{0:T(1024)S(1)} %get-tuple-element.78), kind=kCustom, calls=%fused_computation.clone | custom fusion | bytes 2101248 | tf_op jit(solution)/shard_map/jit(_take)/gather | solution.py:77
  46.1 2.7 broadcast_select_fusion.5
  50.6 3.1 fusion.52
  53.7 2.5 fusion.38
  56.2 3.3 convolution_multiply_fusion.2
  60.6 5.1 %gather_fusion.5 = bf16[1024,512]{1,0:T(8,128)(2,1)} fusion(bf16[256,512]{1,0:T(8,128)(2,1)S(1)} %bitcast.154, s32[1024]{0:T(1024)S(1)} %get-tuple-element.86), kind=kCustom, calls=%fused_computation.3.clone | custom fusion | bytes 2101248 | tf_op jit(solution)/shard_map/while/body/eval_jaxpr/jit(_take)/gather | solution.py:113
  65.7 2.4 broadcast_select_fusion.4
  69.1 5.1 %gather_fusion.7 = bf16[1024,512]{1,0:T(8,128)(2,1)} fusion(bf16[256,512]{1,0:T(8,128)(2,1)S(1)} %bitcast.153, s32[1024]{0:T(1024)S(1)} %get-tuple-element.87), kind=kCustom, calls=%fused_computation.4.clone | custom fusion | bytes 2101248 | tf_op jit(solution)/shard_map/while/body/eval_jaxpr/jit(_take)/gather | solution.py:113
  74.2 1.5 broadcast_select_fusion.3
  76.7 3.1 convolution_multiply_fusion
  79.8 3.9 %fusion.6 = f32[2,128,512]{2,0,1:T(2,128)S(1)} fusion(f32[8,128,512]{2,1,0:T(8,128)} %convolution_multiply_fusion, s32[8]{0:T(128)S(1)} %fusion.117), kind=kOutput, calls=%fused_computation.16 | convolution fusion | flops 12582928 | bytes 2621472 | tf_op jit(solution)/shard_map/while/body/eval_jaxpr/qm,qoi->moi/dot_general | solution.py:49
  85.0 3.3 convolution_multiply_fusion.1
  88.4 3.9 %fusion.8 = f32[2,128,512]{2,0,1:T(2,128)S(1)} fusion(f32[8,128,512]{2,1,0:T(8,128)} %convolution_multiply_fusion.1, s32[8]{0:T(128)S(1)} %fusion.116), kind=kOutput, calls=%fused_computation.18 | convolution fusion | flops 12582928 | bytes 2621472 | tf_op jit(solution)/shard_map/while/body/eval_jaxpr/qm,qoi->moi/dot_general | solution.py:49
  92.3 2.5 fusion.24
  95.3 1.6 gather_fusion.2
  96.9 2.8 fusion.34
  99.7 1.6 gather_fusion.3
  101.3 2.0 fusion.36
  103.3 3.5 fusion.50
  106.8 4.2 %add_multiply_fusion = f32[8,128,512]{2,1,0:T(8,128)} fusion(f32[8,128,512]{2,1,0:T(8,128)} %fusion.52, f32[8,128,512]{2,1,0:T(8,128)} %fusion.50, f32[8,128,128]{1,2,0:T(8,128)S(1)} %fusion.36, bf16[8,128,512]{2,1,0:T(8,128)(2,1)S(1)} %copy-done.1, pred[8]{0:T(512)(128)(4,1)S(1)} %get-tuple-element.90, s32[8,128]{1,0:T(8,128)S(1)} %bitcast.180, ...), kind=kOutput, calls=%fused_computation.22 | convolution fusion | flops 137495680 | bytes 7868440 | tf_op jit(solution)/shard_map/while/body/eval_jaxpr/smk,skd->smd/dot_general | solution.py:91
  111.0 7.6 %scatter_custom_fusion = f32[256,512]{1,0:T(8,128)S(1)} fusion(s32[1024]{0:T(1024)S(1)} %bitcast.181, f32[1024,512]{1,0:T(8,128)} %bitcast.159, f32[]{:T(128)} %constant.155.clone.1), kind=kCustom, calls=%fused_computation.124 | custom fusion | flops 524288 | bytes 524800 | tf_op jit(solution)/shard_map/scatter-add | solution.py:143
  123.3 130.5 %all-reduce.3.cloned.1.call-done = f32[512,512]{0,1:T(8,128)} async-done(((f32[512,512]{0,1:T(8,128)}), f32[512,512]{0,1:T(8,128)}) %all-reduce.3.cloned.1.call-update) | async-done | bytes 1048592 | tf_op jit(solution)/shard_map/psum | solution.py:152
  253.7 2.5 copy.16
  256.3 114.1 %all-reduce.5.cloned.1.call-done = f32[1,512,512]{2,1,0:T(8,128)} async-done(((f32[1,512,512]{2,1,0:T(8,128)}), f32[1,512,512]{2,1,0:T(8,128)}) %all-reduce.5.cloned.1.call-update) | async-done | bytes 1048592 | tf_op jit(solution)/shard_map/psum | solution.py:160
  370.3 2.3 copy.32
  (92 shorter events, 17.9 us)
Async XLA Ops:
  7.2 15.0 %copy-start = (bf16[512,512]{1,0:T(8,128)(2,1)S(1)}, bf16[512,512]{1,0:T(8,128)(2,1)}, u32[]{:S(2)}) copy-start(bf16[512,512]{1,0:T(8,128)(2,1)} %param.13) | copy-start | bytes 1572868
  7.2 246.5 %all-reduce.3.cloned.1.call-start = ((), (), s32[]{:S(2)}) async-start(), calls=%async_computation | async-start | bytes 2097152 | tf_op jit(solution)/shard_map/psum | solution.py:152
  8.9 24.7 %collective-permute-start.4 = (s32[8,2]{0,1:T(2,128)S(1)}, s32[8,2]{0,1:T(2,128)S(1)}, u32[]{:S(2)}, u32[]{:S(2)}) collective-permute-start(s32[8,2]{0,1:T(2,128)S(1)} %pad_add_fusion.1), channel_id=1, source_target_pairs={{0,15},{1,0},{2,1},{3,2},{4,3},{5,4},{6,5},{7,6},{8,7},{9,8},{10,9... | collective-permute-start | bytes 200 | tf_op jit(solution)/shard_map/while/body/eval_jaxpr/ppermute | solution.py:13
  15.9 17.7 %collective-permute-start.2 = (s32[8,2]{0,1:T(2,128)S(1)}, s32[8,2]{0,1:T(2,128)S(1)}, u32[]{:S(2)}, u32[]{:S(2)}) collective-permute-start(s32[8,2]{0,1:T(2,128)S(1)} %pad_add_fusion.1), channel_id=1, source_target_pairs={{0,1},{1,2},{2,3},{3,4},{4,5},{5,6},{6,7},{7,8},{8,9},{9,10},{10,1... | collective-permute-start | bytes 200 | tf_op jit(solution)/shard_map/while/body/eval_jaxpr/ppermute | solution.py:13
  16.6 20.3 %collective-permute-start.5 = (s32[8,256]{1,0:T(8,128)S(1)}, s32[8,256]{1,0:T(8,128)S(1)}, u32[]{:S(2)}, u32[]{:S(2)}) collective-permute-start(s32[8,256]{1,0:T(8,128)S(1)} %pad_add_fusion), channel_id=1, source_target_pairs={{0,15},{1,0},{2,1},{3,2},{4,3},{5,4},{6,5},{7,6},{8,7},{9,8},{10,9... | collective-permute-start | bytes 24584 | tf_op jit(solution)/shard_map/while/body/eval_jaxpr/ppermute | solution.py:13
  22.2 14.7 %collective-permute-start.3 = (s32[8,256]{1,0:T(8,128)S(1)}, s32[8,256]{1,0:T(8,128)S(1)}, u32[]{:S(2)}, u32[]{:S(2)}) collective-permute-start(s32[8,256]{1,0:T(8,128)S(1)} %pad_add_fusion), channel_id=1, source_target_pairs={{0,1},{1,2},{2,3},{3,4},{4,5},{5,6},{6,7},{7,8},{8,9},{9,10},{10,1... | collective-permute-start | bytes 24584 | tf_op jit(solution)/shard_map/while/body/eval_jaxpr/ppermute | solution.py:13
  23.5 8.1 %copy-start.15 = (s32[1,2,4]{2,1,0:T(2,128)S(1)}, s32[1,2,4]{2,1,0:T(2,128)}, u32[]{:S(2)}) copy-start(s32[1,2,4]{2,1,0:T(2,128)} %param.14) | copy-start | bytes 100
  23.5 8.4 %copy-start.11 = (s32[1,2,4,128]{3,2,1,0:T(4,128)S(1)}, s32[1,2,4,128]{3,2,1,0:T(4,128)}, u32[]{:S(2)}) copy-start(s32[1,2,4,128]{3,2,1,0:T(4,128)} %param.16) | copy-start | bytes 12292
  26.0 42.1 %collective-permute-start.1 = (bf16[2,2,128,512]{3,2,1,0:T(8,128)(2,1)}, bf16[2,2,128,512]{3,2,1,0:T(8,128)(2,1)}, u32[]{:S(2)}, u32[]{:S(2)}) collective-permute-start(bf16[2,2,128,512]{3,2,1,0:T(8,128)(2,1)} %pad_maximum_fusion), channel_id=1, source_target_pairs={{0,15},{1,0},{2,1},{3,2},{4,3},{5,4},{6,5},{7,6},{8,7},{9,8},{10,9... | collective-permute-start | bytes 1572872 | tf_op jit(solution)/shard_map/while/body/eval_jaxpr/ppermute | solution.py:13
  33.5 26.0 %collective-permute-start = (bf16[2,2,128,512]{3,2,1,0:T(8,128)(2,1)}, bf16[2,2,128,512]{3,2,1,0:T(8,128)(2,1)}, u32[]{:S(2)}, u32[]{:S(2)}) collective-permute-start(bf16[2,2,128,512]{3,2,1,0:T(8,128)(2,1)} %pad_maximum_fusion), channel_id=1, source_target_pairs={{0,1},{1,2},{2,3},{3,4},{4,5},{5,6},{6,7},{7,8},{8,9},{9,10},{10,1... | collective-permute-start | bytes 1572872 | tf_op jit(solution)/shard_map/while/body/eval_jaxpr/ppermute | solution.py:13
  36.9 22.7 %copy-start.12 = (s32[8,256]{1,0:T(8,128)}, s32[8,256]{1,0:T(8,128)S(1)}, u32[]{:S(2)}) copy-start(s32[8,256]{1,0:T(8,128)S(1)} %collective-permute-done.5) | copy-start | bytes 24580
  36.9 22.7 %copy-start.13 = (s32[8,256]{1,0:T(8,128)}, s32[8,256]{1,0:T(8,128)S(1)}, u32[]{:S(2)}) copy-start(s32[8,256]{1,0:T(8,128)S(1)} %collective-permute-done.3) | copy-start | bytes 24580
  46.1 2.7 copy-start.5
  48.8 1.3 copy-start.10
  48.8 1.8 copy-start.6
  48.8 1.8 copy-start.14
  74.2 1.5 copy-start.4
  75.7 1.0 copy-start.9
  75.8 1.0 slice-start
  79.8 3.9 %copy-start.3 = (bf16[8,128,512]{2,1,0:T(8,128)(2,1)S(1)}, bf16[8,128,512]{2,1,0:T(8,128)(2,1)}, u32[]{:S(2)}) copy-start(bf16[8,128,512]{2,1,0:T(8,128)(2,1)} %gather_fusion.6) | copy-start | bytes 3145732
  79.8 3.9 %copy-start.8 = (bf16[1024,512]{1,0:T(8,128)(2,1)S(1)}, bf16[1024,512]{1,0:T(8,128)(2,1)}, u32[]{:S(2)}) copy-start(bf16[1024,512]{1,0:T(8,128)(2,1)} %broadcast_select_fusion.4) | copy-start | bytes 3145732
  83.7 1.3 slice-start.1
  88.4 3.9 %copy-start.2 = (f32[8,128,512]{2,1,0:T(8,128)S(1)}, f32[8,128,512]{2,1,0:T(8,128)}, u32[]{:S(2)}) copy-start(f32[8,128,512]{2,1,0:T(8,128)} %convolution_multiply_fusion.2) | copy-start | bytes 6291460
  103.3 3.5 copy-start.1
  111.0 9.2 %copy-start.7 = (bf16[1,256,512]{2,1,0:T(8,128)(2,1)S(1)}, bf16[1,256,512]{2,1,0:T(8,128)(2,1)}, u32[]{:S(2)}) copy-start(bf16[1,256,512]{2,1,0:T(8,128)(2,1)} %param.12) | copy-start | bytes 786436
  121.5 248.8 %all-reduce.5.cloned.1.call-start = ((), (), s32[]{:S(2)}) async-start(), calls=%async_computation.1 | async-start | bytes 2097152 | tf_op jit(solution)/shard_map/psum | solution.py:160
Sparse Core Ops, SparseCore 0:
  121.7 132.0 all-reduce.2
  259.0 111.2 all-reduce.4
where the time goes:
time: 380 us; the launch traced here: 379 us
  waiting for transfers between devices  245 us (64%)
  matrix products  48.3 us (13%)
  local copies, waits for them, and re-layouts  36.3 us (10%)
  starting transfers between devices  18.3 us (5%)
  other arithmetic  17.5 us (5%)
  between operations  14.4 us (4%)
    psum x1, waiting for transfers between devices, body(): weight_grad = lax.psum(weight_part, ('grp', 'blk'))  130 us
    psum x1, waiting for transfers between devices, body(): covariance = lax.psum(moment, 'blk')  114 us
    ppermute x6, starting transfers between devices, from_behind(): lax.ppermute(shard, axis, [(i, (i + by) % count) for i in range(count)])  18.2 us
    gather x3, local copies, waits for them, and re-layouts, target_slots(): jnp.take(kept_source_rows.reshape(local_points, feature_width), gather_ro...  14.1 us
    dot_general x3, matrix products, source_slots(): jnp.einsum('smk,skd->smd', linear_weights, candidate_stack, preferred_ele...  10.8 us
    dot_general x6, matrix products, pair_weights(): jnp.einsum('smd,skd->smk', anchor_stack, candidate_stack, preferred_eleme...  10.5 us
    dot_general x3, matrix products, spread_blocks(): jnp.einsum('qm,qoi->moi', choice_mask, slot_pieces, precision=lax.Precisi...  10.3 us
    dot_general x3, matrix products, spread_blocks(): jnp.einsum('smk,smd->skd', linear_weights, anchor_stack, preferred_elemen...  9.73 us
  transfers between devices with their start and end apart: 8, of which 2 were waited for; matrix products, arithmetic and copies ran while one was open for 12% of the time, Pallas kernels for 0%

commit v1 on v0

--- a/solution.py
+++ b/solution.py
@@ -149,7 +149,8 @@
     weight_part = weight_part + lax.dot_general(
         tgt_rows, tgt_grad, (((0,), (0,)), ((), ())), preferred_element_type=jnp.float32
     )
-    weight_grad = lax.psum(weight_part, ("grp", "blk"))
+    one_axis = lax.psum(weight_part, "blk")
+    weight_grad = lax.psum(one_axis, "grp")
     moment = lax.dot_general(
         src_half, src_half, (((0,), (0,)), ((), ())), preferred_element_type=jnp.float32
     )

time: 380 us -> 275 us (0.72)
  waiting for transfers between devices: 245 us -> 149 us
  local copies, waits for them, and re-layouts: 36.3 us -> 30.9 us
    psum x2, waiting for transfers between devices: 245 us -> 149 us  [the longest x1 128 us: body(): one_axis = lax.psum(weight_part, 'blk')]
  transfers between devices with their start and end apart: 8 -> 8, of which waited for: 2 -> 2; matrix products, arithmetic and copies ran while one was open for 12% -> 14% of each run, Pallas kernels for 0% -> 0%
where the time goes in v1:
time: 275 us; the launch traced here: 274 us
  waiting for transfers between devices  149 us (54%)
  matrix products  45.9 us (17%)
  local copies, waits for them, and re-layouts  30.9 us (11%)
  starting transfers between devices  18.3 us (7%)
  other arithmetic  15 us (5%)
  between operations  14.4 us (5%)
    psum x1, waiting for transfers between devices, body(): one_axis = lax.psum(weight_part, 'blk')  128 us
    psum x1, waiting for transfers between devices, body(): weight_grad = lax.psum(one_axis, 'grp')  21 us
    ppermute x6, starting transfers between devices, from_behind(): lax.ppermute(shard, axis, [(i, (i + by) % count) for i in range(count)])  18.2 us
    gather x3, local copies, waits for them, and re-layouts, target_slots(): jnp.take(kept_source_rows.reshape(local_points, feature_width), gather_ro...  12.1 us
    dot_general x3, matrix products, source_slots(): jnp.einsum('smk,skd->smd', linear_weights, candidate_stack, preferred_ele...  10.8 us
    dot_general x3, matrix products, spread_blocks(): jnp.einsum('qm,qoi->moi', choice_mask, slot_pieces, precision=lax.Precisi...  10.3 us
    dot_general x3, matrix products, spread_blocks(): jnp.einsum('smk,smd->skd', linear_weights, anchor_stack, preferred_elemen...  9.42 us
    dot_general x6, matrix products, pair_weights(): jnp.einsum('smd,skd->smk', anchor_stack, candidate_stack, preferred_eleme...  9.42 us
  transfers between devices with their start and end apart: 8, of which 2 were waited for; matrix products, arithmetic and copies ran while one was open for 14% of the time, Pallas kernels for 0%

profile of v1, /device:TPU:0, one launch (start us, length us, event | category | flops | bytes accessed | tf_op | source)
XLA Modules:
  0.0 273.8 jit_solution(10170104762988953560)
XLA Ops:
  8.9 7.0 %collective-permute-start.4 = (s32[8,2]{0,1:T(2,128)S(1)}, s32[8,2]{0,1:T(2,128)S(1)}, u32[]{:S(2)}, u32[]{:S(2)}) collective-permute-start(s32[8,2]{0,1:T(2,128)S(1)} %pad_add_fusion.1), channel_id=1, source_target_pairs={{0,15},{1,0},{2,1},{3,2},{4,3},{5,4},{6,5},{7,6},{8,7},{9,8},{10,9... | collective-permute-start | bytes 200 | tf_op jit(solution)/shard_map/while/body/eval_jaxpr/ppermute | solution.py:13
  16.6 5.6 %collective-permute-start.5 = (s32[8,256]{1,0:T(8,128)S(1)}, s32[8,256]{1,0:T(8,128)S(1)}, u32[]{:S(2)}, u32[]{:S(2)}) collective-permute-start(s32[8,256]{1,0:T(8,128)S(1)} %pad_add_fusion), channel_id=1, source_target_pairs={{0,15},{1,0},{2,1},{3,2},{4,3},{5,4},{6,5},{7,6},{8,7},{9,8},{10,9... | collective-permute-start | bytes 24584 | tf_op jit(solution)/shard_map/while/body/eval_jaxpr/ppermute | solution.py:13
  22.2 1.3 multiply_reduce_fusion.2
  23.5 1.3 multiply_reduce_fusion.1
  26.0 5.6 %collective-permute-start.1 = (bf16[2,2,128,512]{3,2,1,0:T(8,128)(2,1)}, bf16[2,2,128,512]{3,2,1,0:T(8,128)(2,1)}, u32[]{:S(2)}, u32[]{:S(2)}) collective-permute-start(bf16[2,2,128,512]{3,2,1,0:T(8,128)(2,1)} %pad_maximum_fusion), channel_id=1, source_target_pairs={{0,15},{1,0},{2,1},{3,2},{4,3},{5,4},{6,5},{7,6},{8,7},{9,8},{10,9... | collective-permute-start | bytes 1572872 | tf_op jit(solution)/shard_map/while/body/eval_jaxpr/ppermute | solution.py:13
  32.1 1.3 fusion.13
  33.6 1.6 gather_fusion.1
  35.3 1.6 gather_fusion.8
  36.8 1.7 gather_fusion.6
  38.6 4.0 %gather_fusion.4 = bf16[1024,512]{1,0:T(8,128)(2,1)S(1)} fusion(bf16[256,512]{1,0:T(8,128)(2,1)S(1)} %multiply_convert_fusion.2, s32[1024]{0:T(1024)S(1)} %get-tuple-element.79), kind=kCustom, calls=%fused_computation.2.clone | custom fusion | bytes 2101248 | tf_op jit(solution)/shard_map/jit(_take)/gather | solution.py:113
  42.6 5.1 %gather_fusion = bf16[1024,512]{1,0:T(8,128)(2,1)} fusion(bf16[256,512]{1,0:T(8,128)(2,1)S(1)} %multiply_convert_fusion.2, s32[1024]{0:T(1024)S(1)} %get-tuple-element.80), kind=kCustom, calls=%fused_computation.clone | custom fusion | bytes 2101248 | tf_op jit(solution)/shard_map/jit(_take)/gather | solution.py:77
  47.7 2.7 broadcast_select_fusion.5
  50.4 1.3 fusion.32
  52.2 3.1 %fusion.52 = f32[8,128,512]{2,1,0:T(8,128)} fusion(f32[8,128,128]{1,2,0:T(8,128)} %fusion.32, s32[8,128]{1,0:T(8,128)S(1)} %bitcast.177, bf16[8]{0:T(256)(128)(2,1)S(1)} %get-tuple-element.85, bf16[8,128,512]{2,1,0:T(8,128)(2,1)S(1)} %copy-done.5, pred[8]{0:T(512)(128)(4,1)S(1)} %get-tuple-element.92), kind=kOutput, calls=%fused_computation.70 | convolution fusion | flops 135922816 | bytes 3674136 | tf_op jit(solution)/shard_map/smk,skd->smd/dot_general | solution.py:91
  55.3 2.5 fusion.38
  57.8 3.3 %convolution_multiply_fusion.2 = f32[8,128,512]{2,1,0:T(8,128)} fusion(bf16[8,128,512]{2,1,0:T(8,128)(2,1)} %bitcast.168, f32[8,128,128]{1,2,0:T(8,128)} %fusion.38, s32[8,128]{1,0:T(8,128)S(1)} %bitcast.178, bf16[8]{0:T(256)(128)(2,1)S(1)} %get-tuple-element.46), kind=kOutput, calls=%fused_computation.25 | convolution fusion | flops 135922816 | bytes 3674128 | tf_op jit(solution)/shard_map/smk,smd->skd/dot_general | solution.py:43
  61.2 4.0 %gather_fusion.5 = bf16[1024,512]{1,0:T(8,128)(2,1)S(1)} fusion(bf16[256,512]{1,0:T(8,128)(2,1)S(1)} %bitcast.154, s32[1024]{0:T(1024)S(1)} %get-tuple-element.88), kind=kCustom, calls=%fused_computation.3.clone | custom fusion | bytes 2101248 | tf_op jit(solution)/shard_map/while/body/eval_jaxpr/jit(_take)/gather | solution.py:113
  67.4 4.1 %gather_fusion.7 = bf16[1024,512]{1,0:T(8,128)(2,1)S(1)} fusion(bf16[256,512]{1,0:T(8,128)(2,1)S(1)} %bitcast.153, s32[1024]{0:T(1024)S(1)} %get-tuple-element.89), kind=kCustom, calls=%fused_computation.4.clone | custom fusion | bytes 2101248 | tf_op jit(solution)/shard_map/while/body/eval_jaxpr/jit(_take)/gather | solution.py:113
  73.5 3.0 %convolution_multiply_fusion = f32[8,128,512]{2,1,0:T(8,128)} fusion(bf16[8,128,512]{2,1,0:T(8,128)(2,1)} %bitcast.163, f32[8,128,128]{1,2,0:T(8,128)S(1)} %fusion.42, s32[8,128]{1,0:T(8,128)S(1)} %slice-done, bf16[8]{0:T(256)(128)(2,1)S(1)} %get-tuple-element.82), kind=kOutput, calls=%fused_computation.23 | convolution fusion | flops 135922816 | bytes 3674128 | tf_op jit(solution)/shard_map/while/body/eval_jaxpr/smk,smd->skd/dot_general | solution.py:43
  76.6 3.9 %fusion.6 = f32[2,128,512]{2,0,1:T(2,128)S(1)} fusion(f32[8,128,512]{2,1,0:T(8,128)} %convolution_multiply_fusion, s32[8]{0:T(128)S(1)} %fusion.117), kind=kOutput, calls=%fused_computation.16 | convolution fusion | flops 12582928 | bytes 2621472 | tf_op jit(solution)/shard_map/while/body/eval_jaxpr/qm,qoi->moi/dot_general | solution.py:49
  81.2 3.0 %convolution_multiply_fusion.1 = f32[8,128,512]{2,1,0:T(8,128)} fusion(bf16[8,128,512]{2,1,0:T(8,128)(2,1)} %bitcast.160, f32[8,128,128]{1,2,0:T(8,128)S(1)} %fusion.40, s32[8,128]{1,0:T(8,128)S(1)} %slice-done.1, bf16[8]{0:T(256)(128)(2,1)S(1)} %get-tuple-element.81), kind=kOutput, calls=%fused_computation.24 | convolution fusion | flops 135922816 | bytes 3674128 | tf_op jit(solution)/shard_map/while/body/eval_jaxpr/smk,smd->skd/dot_general | solution.py:43
  84.2 3.9 %fusion.8 = f32[2,128,512]{2,0,1:T(2,128)S(1)} fusion(f32[8,128,512]{2,1,0:T(8,128)} %convolution_multiply_fusion.1, s32[8]{0:T(128)S(1)} %fusion.116), kind=kOutput, calls=%fused_computation.18 | convolution fusion | flops 12582928 | bytes 2621472 | tf_op jit(solution)/shard_map/while/body/eval_jaxpr/qm,qoi->moi/dot_general | solution.py:49
  88.2 2.5 fusion.24
  91.8 2.9 %fusion.34 = f32[8,128,128]{1,2,0:T(8,128)} fusion(bf16[8,128,512]{2,1,0:T(8,128)(2,1)} %bitcast.165, bf16[8,128,512]{2,1,0:T(8,128)(2,1)S(1)} %gather_fusion.2, pred[8]{0:T(512)(128)(4,1)S(1)} %get-tuple-element.92), kind=kOutput, calls=%fused_computation.52 | convolution fusion | flops 135004160 | bytes 2621448 | tf_op jit(solution)/shard_map/while/body/eval_jaxpr/smd,skd->smk/dot_general | solution.py:30
  95.3 1.7 fusion.36
  97.0 3.4 %fusion.50 = f32[8,128,512]{2,1,0:T(8,128)} fusion(f32[8,128,128]{1,2,0:T(8,128)} %fusion.34, bf16[8,128,512]{2,1,0:T(8,128)(2,1)} %copy-done.6, pred[8]{0:T(512)(128)(4,1)S(1)} %get-tuple-element.92, s32[8,128]{1,0:T(8,128)S(1)} %bitcast.179, bf16[8]{0:T(256)(128)(2,1)S(1)} %get-tuple-element.84), kind=kOutput, calls=%fused_computation.68 | convolution fusion | flops 135922816 | bytes 3674136 | tf_op jit(solution)/shard_map/while/body/eval_jaxpr/smk,skd->smd/dot_general | solution.py:91
  100.4 4.2 %add_multiply_fusion = f32[8,128,512]{2,1,0:T(8,128)} fusion(f32[8,128,512]{2,1,0:T(8,128)} %fusion.52, f32[8,128,512]{2,1,0:T(8,128)} %fusion.50, f32[8,128,128]{1,2,0:T(8,128)S(1)} %fusion.36, bf16[8,128,512]{2,1,0:T(8,128)(2,1)S(1)} %gather_fusion.3, pred[8]{0:T(512)(128)(4,1)S(1)} %get-tuple-element.92, s32[8,128]{1,0:T(8,128)S(1)} %bitcast.180, ...), kind=kOutput, calls=%fused_computation.22 | convolution fusion | flops 137495680 | bytes 7868440 | tf_op jit(solution)/shard_map/while/body/eval_jaxpr/smk,skd->smd/dot_general | solution.py:91
  104.7 7.6 %scatter_custom_fusion = f32[256,512]{1,0:T(8,128)S(1)} fusion(s32[1024]{0:T(1024)S(1)} %bitcast.181, f32[1024,512]{1,0:T(8,128)} %bitcast.159, f32[]{:T(128)} %constant.155.clone.1), kind=kCustom, calls=%fused_computation.124 | custom fusion | flops 524288 | bytes 524800 | tf_op jit(solution)/shard_map/scatter-add | solution.py:143
  112.9 1.3 fusion.14
  114.3 128.2 %all-reduce.6.cloned.1.call-done = (f32[512,512]{0,1:T(8,128)}, f32[1,512,512]{2,1,0:T(8,128)}) async-done(((f32[512,512]{0,1:T(8,128)}, f32[1,512,512]{2,1,0:T(8,128)}), (f32[512,512]{0,1:T(8,128)}, f32[1,512,512]{2,1,0:T(8,128)})) %all-reduce.6.cloned.1.call-update) | async-done | bytes 2097168 | tf_op jit(solution)/shard_map/psum | solution.py:152
  242.5 21.0 %all-reduce.4.cloned.1.call-done = f32[512,512]{0,1:T(8,128)} async-done(((f32[512,512]{0,1:T(8,128)}), f32[512,512]{0,1:T(8,128)}) %all-reduce.4.cloned.1.call-update) | async-done | bytes 1048592 | tf_op jit(solution)/shard_map/psum | solution.py:153
  263.5 2.5 copy.16
  (96 shorter events, 13.0 us)
Async XLA Ops:
  7.2 15.0 %copy-start = (bf16[512,512]{1,0:T(8,128)(2,1)S(1)}, bf16[512,512]{1,0:T(8,128)(2,1)}, u32[]{:S(2)}) copy-start(bf16[512,512]{1,0:T(8,128)(2,1)} %param.13) | copy-start | bytes 1572868
  7.2 235.3 %all-reduce.6.cloned.1.call-start = ((), (), s32[]{:S(2)}) async-start(), calls=%async_computation.1 | async-start | bytes 4194304 | tf_op jit(solution)/shard_map/psum | solution.py:152
  8.9 26.3 %collective-permute-start.4 = (s32[8,2]{0,1:T(2,128)S(1)}, s32[8,2]{0,1:T(2,128)S(1)}, u32[]{:S(2)}, u32[]{:S(2)}) collective-permute-start(s32[8,2]{0,1:T(2,128)S(1)} %pad_add_fusion.1), channel_id=1, source_target_pairs={{0,15},{1,0},{2,1},{3,2},{4,3},{5,4},{6,5},{7,6},{8,7},{9,8},{10,9... | collective-permute-start | bytes 200 | tf_op jit(solution)/shard_map/while/body/eval_jaxpr/ppermute | solution.py:13
  15.9 19.3 %collective-permute-start.2 = (s32[8,2]{0,1:T(2,128)S(1)}, s32[8,2]{0,1:T(2,128)S(1)}, u32[]{:S(2)}, u32[]{:S(2)}) collective-permute-start(s32[8,2]{0,1:T(2,128)S(1)} %pad_add_fusion.1), channel_id=1, source_target_pairs={{0,1},{1,2},{2,3},{3,4},{4,5},{5,6},{6,7},{7,8},{8,9},{9,10},{10,1... | collective-permute-start | bytes 200 | tf_op jit(solution)/shard_map/while/body/eval_jaxpr/ppermute | solution.py:13
  16.6 21.9 %collective-permute-start.5 = (s32[8,256]{1,0:T(8,128)S(1)}, s32[8,256]{1,0:T(8,128)S(1)}, u32[]{:S(2)}, u32[]{:S(2)}) collective-permute-start(s32[8,256]{1,0:T(8,128)S(1)} %pad_add_fusion), channel_id=1, source_target_pairs={{0,15},{1,0},{2,1},{3,2},{4,3},{5,4},{6,5},{7,6},{8,7},{9,8},{10,9... | collective-permute-start | bytes 24584 | tf_op jit(solution)/shard_map/while/body/eval_jaxpr/ppermute | solution.py:13
  22.2 16.3 %collective-permute-start.3 = (s32[8,256]{1,0:T(8,128)S(1)}, s32[8,256]{1,0:T(8,128)S(1)}, u32[]{:S(2)}, u32[]{:S(2)}) collective-permute-start(s32[8,256]{1,0:T(8,128)S(1)} %pad_add_fusion), channel_id=1, source_target_pairs={{0,1},{1,2},{2,3},{3,4},{4,5},{5,6},{6,7},{7,8},{8,9},{9,10},{10,1... | collective-permute-start | bytes 24584 | tf_op jit(solution)/shard_map/while/body/eval_jaxpr/ppermute | solution.py:13
  23.5 8.1 %copy-start.17 = (s32[1,2,4]{2,1,0:T(2,128)S(1)}, s32[1,2,4]{2,1,0:T(2,128)}, u32[]{:S(2)}) copy-start(s32[1,2,4]{2,1,0:T(2,128)} %param.14) | copy-start | bytes 100
  26.0 40.4 %collective-permute-start.1 = (bf16[2,2,128,512]{3,2,1,0:T(8,128)(2,1)}, bf16[2,2,128,512]{3,2,1,0:T(8,128)(2,1)}, u32[]{:S(2)}, u32[]{:S(2)}) collective-permute-start(bf16[2,2,128,512]{3,2,1,0:T(8,128)(2,1)} %pad_maximum_fusion), channel_id=1, source_target_pairs={{0,15},{1,0},{2,1},{3,2},{4,3},{5,4},{6,5},{7,6},{8,7},{9,8},{10,9... | collective-permute-start | bytes 1572872 | tf_op jit(solution)/shard_map/while/body/eval_jaxpr/ppermute | solution.py:13
  31.7 1.8 copy-start.13
  35.2 26.0 %collective-permute-start = (bf16[2,2,128,512]{3,2,1,0:T(8,128)(2,1)}, bf16[2,2,128,512]{3,2,1,0:T(8,128)(2,1)S(1)}, u32[]{:S(2)}, u32[]{:S(2)}) collective-permute-start(bf16[2,2,128,512]{3,2,1,0:T(8,128)(2,1)} %pad_maximum_fusion), channel_id=1, source_target_pairs={{0,1},{1,2},{2,3},{3,4},{4,5},{5,6},{6,7},{7,8},{8,9},{9,10},{10,1... | collective-permute-start | bytes 1572872 | tf_op jit(solution)/shard_map/while/body/eval_jaxpr/ppermute | solution.py:13
  38.5 22.7 %copy-start.14 = (s32[8,256]{1,0:T(8,128)}, s32[8,256]{1,0:T(8,128)S(1)}, u32[]{:S(2)}) copy-start(s32[8,256]{1,0:T(8,128)S(1)} %collective-permute-done.5) | copy-start | bytes 24580
  38.5 22.7 %copy-start.15 = (s32[8,256]{1,0:T(8,128)}, s32[8,256]{1,0:T(8,128)S(1)}, u32[]{:S(2)}) copy-start(s32[8,256]{1,0:T(8,128)S(1)} %collective-permute-done.3) | copy-start | bytes 24580
  47.7 2.7 copy-start.4
  50.4 1.3 copy-start.11
  50.4 1.8 copy-start.5
  50.4 1.8 copy-start.16
  71.6 1.4 copy-start.3
  71.8 1.7 copy-start.10
  71.8 1.7 slice-start
  76.6 3.9 %copy-start.2 = (bf16[8,128,512]{2,1,0:T(8,128)(2,1)S(1)}, bf16[8,128,512]{2,1,0:T(8,128)(2,1)}, u32[]{:S(2)}) copy-start(bf16[8,128,512]{2,1,0:T(8,128)(2,1)} %gather_fusion.6) | copy-start | bytes 3145732
  76.6 3.9 %copy-start.9 = (bf16[1024,512]{1,0:T(8,128)(2,1)S(1)}, bf16[1024,512]{1,0:T(8,128)(2,1)}, u32[]{:S(2)}) copy-start(bf16[1024,512]{1,0:T(8,128)(2,1)} %broadcast_select_fusion.4) | copy-start | bytes 3145732
  80.5 0.7 slice-start.1
  84.2 3.9 %copy-start.1 = (f32[8,128,512]{2,1,0:T(8,128)S(1)}, f32[8,128,512]{2,1,0:T(8,128)}, u32[]{:S(2)}) copy-start(f32[8,128,512]{2,1,0:T(8,128)} %convolution_multiply_fusion.2) | copy-start | bytes 6291460
  91.7 2.9 %copy-start.6 = (bf16[8,128,512]{2,1,0:T(8,128)(2,1)}, bf16[8,128,512]{2,1,0:T(8,128)(2,1)S(1)}, u32[]{:S(2)}) copy-start(bf16[8,128,512]{2,1,0:T(8,128)(2,1)S(1)} %gather_fusion.2) | copy-start | bytes 3145732
  100.4 12.0 %copy-start.12 = (bf16[1,256,512]{2,1,0:T(8,128)(2,1)S(1)}, bf16[1,256,512]{2,1,0:T(8,128)(2,1)}, u32[]{:S(2)}) copy-start(bf16[1,256,512]{2,1,0:T(8,128)(2,1)} %param.11) | copy-start | bytes 786436
  104.7 8.3 %copy-start.8 = (bf16[1,256,512]{2,1,0:T(8,128)(2,1)S(1)}, bf16[1,256,512]{2,1,0:T(8,128)(2,1)}, u32[]{:S(2)}) copy-start(bf16[1,256,512]{2,1,0:T(8,128)(2,1)} %param.12) | copy-start | bytes 786436
  114.2 149.3 %all-reduce.4.cloned.1.call-start = ((), (), s32[]{:S(2)}) async-start(), calls=%async_computation | async-start | bytes 2097152 | tf_op jit(solution)/shard_map/psum | solution.py:153
  242.5 23.6 %copy-start.7 = (f32[1,512,512]{2,1,0:T(8,128)S(1)}, f32[1,512,512]{2,1,0:T(8,128)}, u32[]{:S(2)}) copy-start(f32[1,512,512]{2,1,0:T(8,128)} %get-tuple-element.101) | copy-start | bytes 3145732
Sparse Core Ops, SparseCore 0:
  114.4 128.0 all-reduce.5
  244.8 18.6 all-reduce.3
